TPU v7x, 256 devices: a whole 4x4x8 slice. The times are simulated.
256 devices in a mesh: member: 16 (over y, x_hi, core), domain: 16 (over x_lo, z).
Axes of the slice: x: 4 (x_hi: 2, x_lo: 2; x = x_hi * 2 + x_lo), y: 4, z: 8, core: 2. Of those that a mesh axis runs over, the one named last changes fastest.
Arguments:
- state: float32 [16, 4, 512, 512], P('member', None, 'domain'), may hold values from -5 to 5
- perturbation: float32 [16, 4, 512, 512], P('member', None, 'domain'), may hold values from -3 to 3
- parents: int32 [16], replicated, may hold values from 0 to 15
Outputs:
- final_state: float32 [16, 4, 512, 512], P('member', None, 'domain')
- score: float32 [16], P('member')
Inputs may be any that keep to these rules, and one draw needn't show every extreme that they name: `parents`: A member may be the parent of several slots or of none.
All inputs are finite; a program needn't handle non-finite values.
Results may differ from a plain program's by a relative error of at most 0.00002.
Values sent between devices are 32-bit elements; how exact they have to be, the bound alone decides.
A program may use at most 64 MiB of HBM per device.

v0:
```python
import jax
import jax.numpy as jnp
from jax import lax
from jax.sharding import PartitionSpec as P

STEPS = 3
time_step = 0.1
viscous = 0.05
coriolis = 1.0


def with_halo(cells, sides, width):
    for axis, dim in sides:
        count = lax.axis_size(axis)
        ends = count - 1
        head = lax.slice_in_dim(cells, 0, width, axis=dim)
        tail = lax.slice_in_dim(cells, cells.shape[dim] - width, cells.shape[dim], axis=dim)
        cells = jnp.concatenate(
            [
                lax.ppermute(tail, axis, [(i, (i + 1) % count) for i in range(ends)]),
                cells,
                lax.ppermute(head, axis, [((i + 1) % count, i) for i in range(ends)]),
            ],
            axis=dim,
        )
    return cells


def gradients(padded):
    middle = padded[:, 1:-1]
    east = jnp.roll(middle, -1, axis=-1)
    west = jnp.roll(middle, 1, axis=-1)
    return (middle, east, west, padded[:, 2:], padded[:, :-2])


def tendency(padded, start_row, total_rows):
    middle, east, west, north, south = gradients(padded)
    grad_x = (east - west) * 0.5
    grad_y = (north - south) * 0.5
    laplace = east + west + north + south - 4.0 * middle
    depth = 1.0 + padded[0]
    fluxes = jnp.stack([depth * padded[1], depth * padded[2]])
    flux_mid, flux_east, flux_west, flux_north, flux_south = gradients(fluxes)
    count = padded.shape[1] - 2
    global_rows = (start_row + 1 + jnp.arange(count, dtype=jnp.int32)).astype(jnp.float32)
    latitude = coriolis * (2.0 * (global_rows + 0.5) / total_rows - 1.0)
    latitude = latitude[:, None]
    height, speed_u, speed_v, tracer = (middle[0], middle[1], middle[2], middle[3])
    advect = speed_u * grad_x + speed_v * grad_y
    d_eta = (
        -((flux_east[0] - flux_west[0]) * 0.5 + (flux_north[1] - flux_south[1]) * 0.5)
        + viscous * laplace[0]
    )
    d_u = -advect[1] + latitude * speed_v - grad_x[0] + viscous * laplace[1]
    d_v = -advect[2] - latitude * speed_u - grad_y[0] + viscous * laplace[2]
    d_q = -advect[3] + viscous * laplace[3]
    return jnp.stack([d_eta, d_u, d_v, d_q])


def section_operator(field, first_row, total_rows):
    padded = with_halo(field, (("domain", 1),), 1)
    return tendency(padded, first_row - 1, total_rows)


def step_shallow(field, first_row, total_rows):
    start = section_operator(field, first_row, total_rows)
    first = field + time_step * start
    second = 0.75 * field + 0.25 * (
        first + time_step * section_operator(first, first_row, total_rows)
    )
    return 1.0 / 3.0 * field + 2.0 / 3.0 * (
        second + time_step * section_operator(second, first_row, total_rows)
    )


def run_steps(field, first_row, total_rows):
    for count in range(STEPS):
        field = step_shallow(field, first_row, total_rows)
    return field


def on_device(state, perturbation, parents):
    rows = state.shape[2]
    width = state.shape[3]
    total_rows = rows * lax.axis_size("domain")
    first_row = lax.axis_index("domain") * rows
    before = run_steps(state[0], first_row, total_rows)
    global_rows = (first_row + jnp.arange(rows, dtype=jnp.int32)).astype(jnp.float32)
    weight = 1.0 + 2.0 * global_rows / (total_rows - 1)
    local_score = jnp.sum(weight[:, None] * before[3] * before[3])
    score = lax.psum(local_score, "domain") / (total_rows * width)
    parent = lax.dynamic_index_in_dim(parents, lax.axis_index("member"), 0, keepdims=False)
    piece = lax.all_gather(before[None], "member", axis=0, tiled=True)
    count = piece.shape[0]
    inside = (parent >= 0) & (parent < count)
    chosen = lax.dynamic_index_in_dim(piece, jnp.clip(parent, 0, count - 1), 0, keepdims=False)
    cloned = jnp.where(inside, chosen, jnp.zeros_like(before))
    after = run_steps(cloned + perturbation[0], first_row, total_rows)
    return (after[None], jnp.reshape(score, (1,)))


def solution(mesh):
    placed = (P("member", None, "domain", None), P("member", None, "domain", None), P())
    return jax.shard_map(
        on_device,
        mesh=mesh,
        in_specs=placed,
        out_specs=(P("member", None, "domain", None), P("member")),
        check_vma=False,
    )
```

profile of v0, /device:TPU:2, one launch (start us, length us, event | category | flops | bytes accessed | tf_op | source)
XLA Modules:
  0.0 271.7 jit_solution(4103556976015861069)
XLA Ops:
  8.1 3.8 %collective-permute-start = (f32[4,1,512]{2,1,0:T(1,128)S(1)}, f32[4,1,512]{2,1,0:T(1,128)S(1)}, u32[]{:S(2)}, u32[]{:S(2)}) collective-permute-start(f32[4,1,512]{2,1,0:T(1,128)S(1)} %get-tuple-element.324), channel_id=1, source_target_pairs={{0,1},{1,2},{2,3},{3,4},{4,5},{5,6},{6,7},{7,8},{8,9},{9,10},{10,1... | collective-permute-start | bytes 24584 | tf_op jit(solution)/shard_map/ppermute | solution.py:20
  12.0 5.8 %collective-permute-start.1 = (f32[4,1,512]{2,1,0:T(1,128)S(1)}, f32[4,1,512]{2,1,0:T(1,128)S(1)}, u32[]{:S(2)}, u32[]{:S(2)}) collective-permute-start(f32[4,1,512]{2,1,0:T(1,128)S(1)} %get-tuple-element.325), channel_id=1, source_target_pairs={{1,0},{2,1},{3,2},{4,3},{5,4},{6,5},{7,6},{8,7},{9,8},{10,9},{11,1... | collective-permute-start | bytes 24584 | tf_op jit(solution)/shard_map/ppermute | solution.py:22
  25.7 6.0 %collective-permute-start.3 = (f32[4,1,512]{2,1,0:T(1,128)S(1)}, f32[4,1,512]{2,1,0:T(1,128)S(1)}, u32[]{:S(2)}, u32[]{:S(2)}) collective-permute-start(f32[4,1,512]{2,1,0:T(1,128)S(1)} %get-tuple-element.316), channel_id=1, source_target_pairs={{1,0},{2,1},{3,2},{4,3},{5,4},{6,5},{7,6},{8,7},{9,8},{10,9},{11,1... | collective-permute-start | bytes 24584 | tf_op jit(solution)/shard_map/ppermute | solution.py:22
  36.8 5.4 %collective-permute-start.5 = (f32[4,1,512]{2,1,0:T(1,128)S(1)}, f32[4,1,512]{2,1,0:T(1,128)S(1)}, u32[]{:S(2)}, u32[]{:S(2)}) collective-permute-start(f32[4,1,512]{2,1,0:T(1,128)S(1)} %get-tuple-element.307), channel_id=1, source_target_pairs={{1,0},{2,1},{3,2},{4,3},{5,4},{6,5},{7,6},{8,7},{9,8},{10,9},{11,1... | collective-permute-start | bytes 24584 | tf_op jit(solution)/shard_map/ppermute | solution.py:22
  47.9 4.8 %collective-permute-start.7 = (f32[4,1,512]{2,1,0:T(1,128)S(1)}, f32[4,1,512]{2,1,0:T(1,128)S(1)}, u32[]{:S(2)}, u32[]{:S(2)}) collective-permute-start(f32[4,1,512]{2,1,0:T(1,128)S(1)} %get-tuple-element.298), channel_id=1, source_target_pairs={{1,0},{2,1},{3,2},{4,3},{5,4},{6,5},{7,6},{8,7},{9,8},{10,9},{11,1... | collective-permute-start | bytes 24584 | tf_op jit(solution)/shard_map/ppermute | solution.py:22
  58.2 4.9 %collective-permute-start.9 = (f32[4,1,512]{2,1,0:T(1,128)S(1)}, f32[4,1,512]{2,1,0:T(1,128)S(1)}, u32[]{:S(2)}, u32[]{:S(2)}) collective-permute-start(f32[4,1,512]{2,1,0:T(1,128)S(1)} %get-tuple-element.289), channel_id=1, source_target_pairs={{1,0},{2,1},{3,2},{4,3},{5,4},{6,5},{7,6},{8,7},{9,8},{10,9},{11,1... | collective-permute-start | bytes 24584 | tf_op jit(solution)/shard_map/ppermute | solution.py:22
  67.8 5.8 %collective-permute-start.11 = (f32[4,1,512]{2,1,0:T(1,128)S(1)}, f32[4,1,512]{2,1,0:T(1,128)S(1)}, u32[]{:S(2)}, u32[]{:S(2)}) collective-permute-start(f32[4,1,512]{2,1,0:T(1,128)S(1)} %get-tuple-element.280), channel_id=1, source_target_pairs={{1,0},{2,1},{3,2},{4,3},{5,4},{6,5},{7,6},{8,7},{9,8},{10,9},{11,1... | collective-permute-start | bytes 24584 | tf_op jit(solution)/shard_map/ppermute | solution.py:22
  77.8 6.3 %collective-permute-start.13 = (f32[4,1,512]{2,1,0:T(1,128)S(1)}, f32[4,1,512]{2,1,0:T(1,128)S(1)}, u32[]{:S(2)}, u32[]{:S(2)}) collective-permute-start(f32[4,1,512]{2,1,0:T(1,128)S(1)} %get-tuple-element.271), channel_id=1, source_target_pairs={{1,0},{2,1},{3,2},{4,3},{5,4},{6,5},{7,6},{8,7},{9,8},{10,9},{11,1... | collective-permute-start | bytes 24584 | tf_op jit(solution)/shard_map/ppermute | solution.py:22
  88.2 6.3 %collective-permute-start.15 = (f32[4,1,512]{2,1,0:T(1,128)S(1)}, f32[4,1,512]{2,1,0:T(1,128)S(1)}, u32[]{:S(2)}, u32[]{:S(2)}) collective-permute-start(f32[4,1,512]{2,1,0:T(1,128)S(1)} %get-tuple-element.262), channel_id=1, source_target_pairs={{1,0},{2,1},{3,2},{4,3},{5,4},{6,5},{7,6},{8,7},{9,8},{10,9},{11,1... | collective-permute-start | bytes 24584 | tf_op jit(solution)/shard_map/ppermute | solution.py:22
  98.7 6.4 %collective-permute-start.17 = (f32[4,1,512]{2,1,0:T(1,128)S(1)}, f32[4,1,512]{2,1,0:T(1,128)S(1)}, u32[]{:S(2)}, u32[]{:S(2)}) collective-permute-start(f32[4,1,512]{2,1,0:T(1,128)S(1)} %get-tuple-element.253), channel_id=1, source_target_pairs={{1,0},{2,1},{3,2},{4,3},{5,4},{6,5},{7,6},{8,7},{9,8},{10,9},{11,1... | collective-permute-start | bytes 24584 | tf_op jit(solution)/shard_map/ppermute | solution.py:22
  111.5 35.7 %psum.7 = f32[]{:T(128)} all-reduce(f32[]{:T(128)} %fusion.150), channel_id=1, replica_groups=mesh['member'=16,'domain'=16] {'domain'}, use_global_device_ids=true, to_apply=%region_1.2 | all-reduce | flops 1 | bytes 8 | tf_op jit(solution)/shard_map/psum | solution.py:91
  147.9 19.7 %all-gather.2.cloned.1.call-done = f32[16,4,32,512]{3,2,1,0:T(8,128)} async-done(((f32[1,4,32,512]{3,2,1,0:T(8,128)}), f32[16,4,32,512]{3,2,1,0:T(8,128)}) %all-gather.2.cloned.1.call-update) | async-done | bytes 4194320 | tf_op jit(solution)/shard_map/all_gather | solution.py:93
  168.7 3.5 %collective-permute-start.18 = (f32[4,1,512]{2,1,0:T(1,128)S(1)}, f32[4,1,512]{2,1,0:T(1,128)S(1)}, u32[]{:S(2)}, u32[]{:S(2)}) collective-permute-start(f32[4,1,512]{2,1,0:T(1,128)S(1)} %get-tuple-element.243), channel_id=1, source_target_pairs={{0,1},{1,2},{2,3},{3,4},{4,5},{5,6},{6,7},{7,8},{8,9},{9,10},{10,1... | collective-permute-start | bytes 24584 | tf_op jit(solution)/shard_map/ppermute | solution.py:20
  172.2 4.6 %collective-permute-start.19 = (f32[4,1,512]{2,1,0:T(1,128)S(1)}, f32[4,1,512]{2,1,0:T(1,128)S(1)}, u32[]{:S(2)}, u32[]{:S(2)}) collective-permute-start(f32[4,1,512]{2,1,0:T(1,128)S(1)} %get-tuple-element.244), channel_id=1, source_target_pairs={{1,0},{2,1},{3,2},{4,3},{5,4},{6,5},{7,6},{8,7},{9,8},{10,9},{11,1... | collective-permute-start | bytes 24584 | tf_op jit(solution)/shard_map/ppermute | solution.py:22
  182.0 5.1 %collective-permute-start.21 = (f32[4,1,512]{2,1,0:T(1,128)S(1)}, f32[4,1,512]{2,1,0:T(1,128)S(1)}, u32[]{:S(2)}, u32[]{:S(2)}) collective-permute-start(f32[4,1,512]{2,1,0:T(1,128)S(1)} %get-tuple-element.235), channel_id=1, source_target_pairs={{1,0},{2,1},{3,2},{4,3},{5,4},{6,5},{7,6},{8,7},{9,8},{10,9},{11,1... | collective-permute-start | bytes 24584 | tf_op jit(solution)/shard_map/ppermute | solution.py:22
  189.4 4.5 %collective-permute-start.22 = (f32[4,1,512]{2,1,0:T(1,128)S(1)}, f32[4,1,512]{2,1,0:T(1,128)S(1)}, u32[]{:S(2)}, u32[]{:S(2)}) collective-permute-start(f32[4,1,512]{2,1,0:T(1,128)S(1)} %get-tuple-element.225), channel_id=1, source_target_pairs={{0,1},{1,2},{2,3},{3,4},{4,5},{5,6},{6,7},{7,8},{8,9},{9,10},{10,1... | collective-permute-start | bytes 24584 | tf_op jit(solution)/shard_map/ppermute | solution.py:20
  193.9 3.7 %collective-permute-start.23 = (f32[4,1,512]{2,1,0:T(1,128)S(1)}, f32[4,1,512]{2,1,0:T(1,128)S(1)}, u32[]{:S(2)}, u32[]{:S(2)}) collective-permute-start(f32[4,1,512]{2,1,0:T(1,128)S(1)} %get-tuple-element.226), channel_id=1, source_target_pairs={{1,0},{2,1},{3,2},{4,3},{5,4},{6,5},{7,6},{8,7},{9,8},{10,9},{11,1... | collective-permute-start | bytes 24584 | tf_op jit(solution)/shard_map/ppermute | solution.py:22
  200.4 3.9 %collective-permute-start.24 = (f32[4,1,512]{2,1,0:T(1,128)S(1)}, f32[4,1,512]{2,1,0:T(1,128)S(1)}, u32[]{:S(2)}, u32[]{:S(2)}) collective-permute-start(f32[4,1,512]{2,1,0:T(1,128)S(1)} %get-tuple-element.216), channel_id=1, source_target_pairs={{0,1},{1,2},{2,3},{3,4},{4,5},{5,6},{6,7},{7,8},{8,9},{9,10},{10,1... | collective-permute-start | bytes 24584 | tf_op jit(solution)/shard_map/ppermute | solution.py:20
  204.3 4.0 %collective-permute-start.25 = (f32[4,1,512]{2,1,0:T(1,128)S(1)}, f32[4,1,512]{2,1,0:T(1,128)S(1)}, u32[]{:S(2)}, u32[]{:S(2)}) collective-permute-start(f32[4,1,512]{2,1,0:T(1,128)S(1)} %get-tuple-element.217), channel_id=1, source_target_pairs={{1,0},{2,1},{3,2},{4,3},{5,4},{6,5},{7,6},{8,7},{9,8},{10,9},{11,1... | collective-permute-start | bytes 24584 | tf_op jit(solution)/shard_map/ppermute | solution.py:22
  213.8 5.1 %collective-permute-start.27 = (f32[4,1,512]{2,1,0:T(1,128)S(1)}, f32[4,1,512]{2,1,0:T(1,128)S(1)}, u32[]{:S(2)}, u32[]{:S(2)}) collective-permute-start(f32[4,1,512]{2,1,0:T(1,128)S(1)} %get-tuple-element.208), channel_id=1, source_target_pairs={{1,0},{2,1},{3,2},{4,3},{5,4},{6,5},{7,6},{8,7},{9,8},{10,9},{11,1... | collective-permute-start | bytes 24584 | tf_op jit(solution)/shard_map/ppermute | solution.py:22
  223.4 5.8 %collective-permute-start.29 = (f32[4,1,512]{2,1,0:T(1,128)S(1)}, f32[4,1,512]{2,1,0:T(1,128)S(1)}, u32[]{:S(2)}, u32[]{:S(2)}) collective-permute-start(f32[4,1,512]{2,1,0:T(1,128)S(1)} %get-tuple-element.199), channel_id=1, source_target_pairs={{1,0},{2,1},{3,2},{4,3},{5,4},{6,5},{7,6},{8,7},{9,8},{10,9},{11,1... | collective-permute-start | bytes 24584 | tf_op jit(solution)/shard_map/ppermute | solution.py:22
  233.4 6.3 %collective-permute-start.31 = (f32[4,1,512]{2,1,0:T(1,128)S(1)}, f32[4,1,512]{2,1,0:T(1,128)S(1)}, u32[]{:S(2)}, u32[]{:S(2)}) collective-permute-start(f32[4,1,512]{2,1,0:T(1,128)S(1)} %get-tuple-element.190), channel_id=1, source_target_pairs={{1,0},{2,1},{3,2},{4,3},{5,4},{6,5},{7,6},{8,7},{9,8},{10,9},{11,1... | collective-permute-start | bytes 24584 | tf_op jit(solution)/shard_map/ppermute | solution.py:22
  243.8 6.3 %collective-permute-start.33 = (f32[4,1,512]{2,1,0:T(1,128)S(1)}, f32[4,1,512]{2,1,0:T(1,128)S(1)}, u32[]{:S(2)}, u32[]{:S(2)}) collective-permute-start(f32[4,1,512]{2,1,0:T(1,128)S(1)} %get-tuple-element.181), channel_id=1, source_target_pairs={{1,0},{2,1},{3,2},{4,3},{5,4},{6,5},{7,6},{8,7},{9,8},{10,9},{11,1... | collective-permute-start | bytes 24584 | tf_op jit(solution)/shard_map/ppermute | solution.py:22
  254.3 6.3 %collective-permute-start.35 = (f32[4,1,512]{2,1,0:T(1,128)S(1)}, f32[4,1,512]{2,1,0:T(1,128)S(1)}, u32[]{:S(2)}, u32[]{:S(2)}) collective-permute-start(f32[4,1,512]{2,1,0:T(1,128)S(1)} %get-tuple-element.172), channel_id=1, source_target_pairs={{1,0},{2,1},{3,2},{4,3},{5,4},{6,5},{7,6},{8,7},{9,8},{10,9},{11,1... | collective-permute-start | bytes 24584 | tf_op jit(solution)/shard_map/ppermute | solution.py:22
  (243 shorter events, 82.3 us)
Async XLA Ops:
  7.2 160.4 %all-gather.2.cloned.1.call-start = ((), (), s32[]{:S(2)}) async-start(), calls=%async_computation | async-start | bytes 4456448 | tf_op jit(solution)/shard_map/all_gather | solution.py:93
  8.1 12.7 %collective-permute-start = (f32[4,1,512]{2,1,0:T(1,128)S(1)}, f32[4,1,512]{2,1,0:T(1,128)S(1)}, u32[]{:S(2)}, u32[]{:S(2)}) collective-permute-start(f32[4,1,512]{2,1,0:T(1,128)S(1)} %get-tuple-element.324), channel_id=1, source_target_pairs={{0,1},{1,2},{2,3},{3,4},{4,5},{5,6},{6,7},{7,8},{8,9},{9,10},{10,1... | collective-permute-start | bytes 24584 | tf_op jit(solution)/shard_map/ppermute | solution.py:20
  12.0 8.9 %collective-permute-start.1 = (f32[4,1,512]{2,1,0:T(1,128)S(1)}, f32[4,1,512]{2,1,0:T(1,128)S(1)}, u32[]{:S(2)}, u32[]{:S(2)}) collective-permute-start(f32[4,1,512]{2,1,0:T(1,128)S(1)} %get-tuple-element.325), channel_id=1, source_target_pairs={{1,0},{2,1},{3,2},{4,3},{5,4},{6,5},{7,6},{8,7},{9,8},{10,9},{11,1... | collective-permute-start | bytes 24584 | tf_op jit(solution)/shard_map/ppermute | solution.py:22
  23.8 8.1 %collective-permute-start.2 = (f32[4,1,512]{2,1,0:T(1,128)S(1)}, f32[4,1,512]{2,1,0:T(1,128)S(1)}, u32[]{:S(2)}, u32[]{:S(2)}) collective-permute-start(f32[4,1,512]{2,1,0:T(1,128)S(1)} %get-tuple-element.315), channel_id=1, source_target_pairs={{0,1},{1,2},{2,3},{3,4},{4,5},{5,6},{6,7},{7,8},{8,9},{9,10},{10,1... | collective-permute-start | bytes 24584 | tf_op jit(solution)/shard_map/ppermute | solution.py:20
  34.0 8.3 %collective-permute-start.4 = (f32[4,1,512]{2,1,0:T(1,128)S(1)}, f32[4,1,512]{2,1,0:T(1,128)S(1)}, u32[]{:S(2)}, u32[]{:S(2)}) collective-permute-start(f32[4,1,512]{2,1,0:T(1,128)S(1)} %get-tuple-element.306), channel_id=1, source_target_pairs={{0,1},{1,2},{2,3},{3,4},{4,5},{5,6},{6,7},{7,8},{8,9},{9,10},{10,1... | collective-permute-start | bytes 24584 | tf_op jit(solution)/shard_map/ppermute | solution.py:20
  44.5 8.3 %collective-permute-start.6 = (f32[4,1,512]{2,1,0:T(1,128)S(1)}, f32[4,1,512]{2,1,0:T(1,128)S(1)}, u32[]{:S(2)}, u32[]{:S(2)}) collective-permute-start(f32[4,1,512]{2,1,0:T(1,128)S(1)} %get-tuple-element.297), channel_id=1, source_target_pairs={{0,1},{1,2},{2,3},{3,4},{4,5},{5,6},{6,7},{7,8},{8,9},{9,10},{10,1... | collective-permute-start | bytes 24584 | tf_op jit(solution)/shard_map/ppermute | solution.py:20
  54.9 8.3 %collective-permute-start.8 = (f32[4,1,512]{2,1,0:T(1,128)S(1)}, f32[4,1,512]{2,1,0:T(1,128)S(1)}, u32[]{:S(2)}, u32[]{:S(2)}) collective-permute-start(f32[4,1,512]{2,1,0:T(1,128)S(1)} %get-tuple-element.288), channel_id=1, source_target_pairs={{0,1},{1,2},{2,3},{3,4},{4,5},{5,6},{6,7},{7,8},{8,9},{9,10},{10,1... | collective-permute-start | bytes 24584 | tf_op jit(solution)/shard_map/ppermute | solution.py:20
  65.4 8.3 %collective-permute-start.10 = (f32[4,1,512]{2,1,0:T(1,128)S(1)}, f32[4,1,512]{2,1,0:T(1,128)S(1)}, u32[]{:S(2)}, u32[]{:S(2)}) collective-permute-start(f32[4,1,512]{2,1,0:T(1,128)S(1)} %get-tuple-element.279), channel_id=1, source_target_pairs={{0,1},{1,2},{2,3},{3,4},{4,5},{5,6},{6,7},{7,8},{8,9},{9,10},{10,1... | collective-permute-start | bytes 24584 | tf_op jit(solution)/shard_map/ppermute | solution.py:20
  75.9 8.3 %collective-permute-start.12 = (f32[4,1,512]{2,1,0:T(1,128)S(1)}, f32[4,1,512]{2,1,0:T(1,128)S(1)}, u32[]{:S(2)}, u32[]{:S(2)}) collective-permute-start(f32[4,1,512]{2,1,0:T(1,128)S(1)} %get-tuple-element.270), channel_id=1, source_target_pairs={{0,1},{1,2},{2,3},{3,4},{4,5},{5,6},{6,7},{7,8},{8,9},{9,10},{10,1... | collective-permute-start | bytes 24584 | tf_op jit(solution)/shard_map/ppermute | solution.py:20
  77.8 7.7 %collective-permute-start.13 = (f32[4,1,512]{2,1,0:T(1,128)S(1)}, f32[4,1,512]{2,1,0:T(1,128)S(1)}, u32[]{:S(2)}, u32[]{:S(2)}) collective-permute-start(f32[4,1,512]{2,1,0:T(1,128)S(1)} %get-tuple-element.271), channel_id=1, source_target_pairs={{1,0},{2,1},{3,2},{4,3},{5,4},{6,5},{7,6},{8,7},{9,8},{10,9},{11,1... | collective-permute-start | bytes 24584 | tf_op jit(solution)/shard_map/ppermute | solution.py:22
  86.3 8.3 %collective-permute-start.14 = (f32[4,1,512]{2,1,0:T(1,128)S(1)}, f32[4,1,512]{2,1,0:T(1,128)S(1)}, u32[]{:S(2)}, u32[]{:S(2)}) collective-permute-start(f32[4,1,512]{2,1,0:T(1,128)S(1)} %get-tuple-element.261), channel_id=1, source_target_pairs={{0,1},{1,2},{2,3},{3,4},{4,5},{5,6},{6,7},{7,8},{8,9},{9,10},{10,1... | collective-permute-start | bytes 24584 | tf_op jit(solution)/shard_map/ppermute | solution.py:20
  96.8 8.5 %collective-permute-start.16 = (f32[4,1,512]{2,1,0:T(1,128)S(1)}, f32[4,1,512]{2,1,0:T(1,128)S(1)}, u32[]{:S(2)}, u32[]{:S(2)}) collective-permute-start(f32[4,1,512]{2,1,0:T(1,128)S(1)} %get-tuple-element.252), channel_id=1, source_target_pairs={{0,1},{1,2},{2,3},{3,4},{4,5},{5,6},{6,7},{7,8},{8,9},{9,10},{10,1... | collective-permute-start | bytes 24584 | tf_op jit(solution)/shard_map/ppermute | solution.py:20
  98.7 7.8 %collective-permute-start.17 = (f32[4,1,512]{2,1,0:T(1,128)S(1)}, f32[4,1,512]{2,1,0:T(1,128)S(1)}, u32[]{:S(2)}, u32[]{:S(2)}) collective-permute-start(f32[4,1,512]{2,1,0:T(1,128)S(1)} %get-tuple-element.253), channel_id=1, source_target_pairs={{1,0},{2,1},{3,2},{4,3},{5,4},{6,5},{7,6},{8,7},{9,8},{10,9},{11,1... | collective-permute-start | bytes 24584 | tf_op jit(solution)/shard_map/ppermute | solution.py:22
  168.7 8.1 %collective-permute-start.18 = (f32[4,1,512]{2,1,0:T(1,128)S(1)}, f32[4,1,512]{2,1,0:T(1,128)S(1)}, u32[]{:S(2)}, u32[]{:S(2)}) collective-permute-start(f32[4,1,512]{2,1,0:T(1,128)S(1)} %get-tuple-element.243), channel_id=1, source_target_pairs={{0,1},{1,2},{2,3},{3,4},{4,5},{5,6},{6,7},{7,8},{8,9},{9,10},{10,1... | collective-permute-start | bytes 24584 | tf_op jit(solution)/shard_map/ppermute | solution.py:20
  179.0 8.3 %collective-permute-start.20 = (f32[4,1,512]{2,1,0:T(1,128)S(1)}, f32[4,1,512]{2,1,0:T(1,128)S(1)}, u32[]{:S(2)}, u32[]{:S(2)}) collective-permute-start(f32[4,1,512]{2,1,0:T(1,128)S(1)} %get-tuple-element.234), channel_id=1, source_target_pairs={{0,1},{1,2},{2,3},{3,4},{4,5},{5,6},{6,7},{7,8},{8,9},{9,10},{10,1... | collective-permute-start | bytes 24584 | tf_op jit(solution)/shard_map/ppermute | solution.py:20
  189.4 8.3 %collective-permute-start.22 = (f32[4,1,512]{2,1,0:T(1,128)S(1)}, f32[4,1,512]{2,1,0:T(1,128)S(1)}, u32[]{:S(2)}, u32[]{:S(2)}) collective-permute-start(f32[4,1,512]{2,1,0:T(1,128)S(1)} %get-tuple-element.225), channel_id=1, source_target_pairs={{0,1},{1,2},{2,3},{3,4},{4,5},{5,6},{6,7},{7,8},{8,9},{9,10},{10,1... | collective-permute-start | bytes 24584 | tf_op jit(solution)/shard_map/ppermute | solution.py:20
  200.4 8.1 %collective-permute-start.24 = (f32[4,1,512]{2,1,0:T(1,128)S(1)}, f32[4,1,512]{2,1,0:T(1,128)S(1)}, u32[]{:S(2)}, u32[]{:S(2)}) collective-permute-start(f32[4,1,512]{2,1,0:T(1,128)S(1)} %get-tuple-element.216), channel_id=1, source_target_pairs={{0,1},{1,2},{2,3},{3,4},{4,5},{5,6},{6,7},{7,8},{8,9},{9,10},{10,1... | collective-permute-start | bytes 24584 | tf_op jit(solution)/shard_map/ppermute | solution.py:20
  210.7 8.3 %collective-permute-start.26 = (f32[4,1,512]{2,1,0:T(1,128)S(1)}, f32[4,1,512]{2,1,0:T(1,128)S(1)}, u32[]{:S(2)}, u32[]{:S(2)}) collective-permute-start(f32[4,1,512]{2,1,0:T(1,128)S(1)} %get-tuple-element.207), channel_id=1, source_target_pairs={{0,1},{1,2},{2,3},{3,4},{4,5},{5,6},{6,7},{7,8},{8,9},{9,10},{10,1... | collective-permute-start | bytes 24584 | tf_op jit(solution)/shard_map/ppermute | solution.py:20
  221.0 8.3 %collective-permute-start.28 = (f32[4,1,512]{2,1,0:T(1,128)S(1)}, f32[4,1,512]{2,1,0:T(1,128)S(1)}, u32[]{:S(2)}, u32[]{:S(2)}) collective-permute-start(f32[4,1,512]{2,1,0:T(1,128)S(1)} %get-tuple-element.198), channel_id=1, source_target_pairs={{0,1},{1,2},{2,3},{3,4},{4,5},{5,6},{6,7},{7,8},{8,9},{9,10},{10,1... | collective-permute-start | bytes 24584 | tf_op jit(solution)/shard_map/ppermute | solution.py:20
  231.5 8.3 %collective-permute-start.30 = (f32[4,1,512]{2,1,0:T(1,128)S(1)}, f32[4,1,512]{2,1,0:T(1,128)S(1)}, u32[]{:S(2)}, u32[]{:S(2)}) collective-permute-start(f32[4,1,512]{2,1,0:T(1,128)S(1)} %get-tuple-element.189), channel_id=1, source_target_pairs={{0,1},{1,2},{2,3},{3,4},{4,5},{5,6},{6,7},{7,8},{8,9},{9,10},{10,1... | collective-permute-start | bytes 24584 | tf_op jit(solution)/shard_map/ppermute | solution.py:20
  233.4 7.7 %collective-permute-start.31 = (f32[4,1,512]{2,1,0:T(1,128)S(1)}, f32[4,1,512]{2,1,0:T(1,128)S(1)}, u32[]{:S(2)}, u32[]{:S(2)}) collective-permute-start(f32[4,1,512]{2,1,0:T(1,128)S(1)} %get-tuple-element.190), channel_id=1, source_target_pairs={{1,0},{2,1},{3,2},{4,3},{5,4},{6,5},{7,6},{8,7},{9,8},{10,9},{11,1... | collective-permute-start | bytes 24584 | tf_op jit(solution)/shard_map/ppermute | solution.py:22
  241.9 8.3 %collective-permute-start.32 = (f32[4,1,512]{2,1,0:T(1,128)S(1)}, f32[4,1,512]{2,1,0:T(1,128)S(1)}, u32[]{:S(2)}, u32[]{:S(2)}) collective-permute-start(f32[4,1,512]{2,1,0:T(1,128)S(1)} %get-tuple-element.180), channel_id=1, source_target_pairs={{0,1},{1,2},{2,3},{3,4},{4,5},{5,6},{6,7},{7,8},{8,9},{9,10},{10,1... | collective-permute-start | bytes 24584 | tf_op jit(solution)/shard_map/ppermute | solution.py:20
  243.8 7.7 %collective-permute-start.33 = (f32[4,1,512]{2,1,0:T(1,128)S(1)}, f32[4,1,512]{2,1,0:T(1,128)S(1)}, u32[]{:S(2)}, u32[]{:S(2)}) collective-permute-start(f32[4,1,512]{2,1,0:T(1,128)S(1)} %get-tuple-element.181), channel_id=1, source_target_pairs={{1,0},{2,1},{3,2},{4,3},{5,4},{6,5},{7,6},{8,7},{9,8},{10,9},{11,1... | collective-permute-start | bytes 24584 | tf_op jit(solution)/shard_map/ppermute | solution.py:22
  252.4 8.3 %collective-permute-start.34 = (f32[4,1,512]{2,1,0:T(1,128)S(1)}, f32[4,1,512]{2,1,0:T(1,128)S(1)}, u32[]{:S(2)}, u32[]{:S(2)}) collective-permute-start(f32[4,1,512]{2,1,0:T(1,128)S(1)} %get-tuple-element.171), channel_id=1, source_target_pairs={{0,1},{1,2},{2,3},{3,4},{4,5},{5,6},{6,7},{7,8},{8,9},{9,10},{10,1... | collective-permute-start | bytes 24584 | tf_op jit(solution)/shard_map/ppermute | solution.py:20
  (16 other events, 182.6 us)
Sparse Core Ops, SparseCore 0:
  108.4 59.1 all-gather.1
where the time goes:
time: 273 us; the launch traced here: 272 us
  starting transfers between devices  149 us (55%)
  waiting for transfers between devices  41.5 us (15%)
  blocking collectives  35.7 us (13%)
  between operations  19.1 us (7%)
  other arithmetic  18.9 us (7%)
  local copies, waits for them, and re-layouts  7.54 us (3%)
    ppermute x18, starting transfers between devices, with_halo(): lax.ppermute(head, axis, [((i + 1) % count, i) for i in range(ends)])  99.1 us
    ppermute x18, starting transfers between devices, with_halo(): lax.ppermute(tail, axis, [(i, (i + 1) % count) for i in range(ends)])  49.7 us
    psum x1, blocking collectives, on_device(): score = lax.psum(local_score, 'domain') / (total_rows * width)  35.7 us
    ppermute x18, waiting for transfers between devices, with_halo(): lax.ppermute(head, axis, [((i + 1) % count, i) for i in range(ends)])  21.8 us
    all_gather x1, waiting for transfers between devices, on_device(): piece = lax.all_gather(before[None], 'member', axis=0, tiled=True)  19.7 us
    slice x36, local copies, waits for them, and re-layouts, gradients(): east = jnp.roll(middle, -1, axis=-1)  5.76 us
    add x18, other arithmetic, tendency(): advect = speed_u * grad_x + speed_v * grad_y  5.57 us
  transfers between devices with their start and end apart: 37, of which 18 were waited for; matrix products, arithmetic and copies ran while one was open for 2% of the time, Pallas kernels for 0%

commit v1 on v0

--- a/solution.py
+++ b/solution.py
@@ -2,6 +2,7 @@
 import jax.numpy as jnp
 from jax import lax
 from jax.sharding import PartitionSpec as P
+from jax.lax import all_to_all, axis_size
 
 STEPS = 3
 time_step = 0.1
@@ -90,7 +91,9 @@
     local_score = jnp.sum(weight[:, None] * before[3] * before[3])
     score = lax.psum(local_score, "domain") / (total_rows * width)
     parent = lax.dynamic_index_in_dim(parents, lax.axis_index("member"), 0, keepdims=False)
-    piece = lax.all_gather(before[None], "member", axis=0, tiled=True)
+    piece = jnp.concatenate(
+        all_to_all(jnp.stack(axis_size("member") * [before[None]]), "member", 0, 0), axis=0
+    )
     count = piece.shape[0]
     inside = (parent >= 0) & (parent < count)
     chosen = lax.dynamic_index_in_dim(piece, jnp.clip(parent, 0, count - 1), 0, keepdims=False)

time: 273 us -> 263 us (0.963)
  between operations: 19.1 us -> 5.71 us
  waiting for transfers between devices: 41.5 us -> 33 us
  starting transfers between devices: 149 us -> 157 us
    all_gather x1 -> x0, waiting for transfers between devices: 19.7 us -> none  [on_device(): piece = lax.all_gather(before[None], 'member', axis=0, tiled=True)]
    all_to_all x0 -> x1, waiting for transfers between devices: none -> 11.6 us  [on_device(): all_to_all(jnp.stack(axis_size('member') * [before[None]]), 'member', 0, 0)]
    ppermute x18, starting transfers between devices: 99.1 us -> 109 us  [with_halo(): lax.ppermute(head, axis, [((i + 1) % count, i) for i in range(ends)])]
    ppermute x18, starting transfers between devices: 49.7 us -> 40.8 us  [with_halo(): lax.ppermute(tail, axis, [(i, (i + 1) % count) for i in range(ends)])]
    all_to_all x0 -> x1, starting transfers between devices: none -> 6.61 us  [on_device(): all_to_all(jnp.stack(axis_size('member') * [before[None]]), 'member', 0, 0)]
where the time goes in v1:
time: 263 us; the launch traced here: 261 us
  starting transfers between devices  157 us (60%)
  blocking collectives  36.9 us (14%)
  waiting for transfers between devices  33 us (13%)
  other arithmetic  18.9 us (7%)
  local copies, waits for them, and re-layouts  10.2 us (4%)
  between operations  5.71 us (2%)
    ppermute x18, starting transfers between devices, with_halo(): lax.ppermute(head, axis, [((i + 1) % count, i) for i in range(ends)])  109 us
    ppermute x18, starting transfers between devices, with_halo(): lax.ppermute(tail, axis, [(i, (i + 1) % count) for i in range(ends)])  40.8 us
    psum x1, blocking collectives, on_device(): score = lax.psum(local_score, 'domain') / (total_rows * width)  36.9 us
    ppermute x18, waiting for transfers between devices, with_halo(): lax.ppermute(head, axis, [((i + 1) % count, i) for i in range(ends)])  21.4 us
    all_to_all x1, waiting for transfers between devices, on_device(): all_to_all(jnp.stack(axis_size('member') * [before[None]]), 'member', 0, 0)  11.6 us
    all_to_all x1, starting transfers between devices, on_device(): all_to_all(jnp.stack(axis_size('member') * [before[None]]), 'member', 0, 0)  6.61 us
    slice x36, local copies, waits for them, and re-layouts, gradients(): east = jnp.roll(middle, -1, axis=-1)  5.77 us
    add x18, other arithmetic, tendency(): advect = speed_u * grad_x + speed_v * grad_y  5.5 us
  transfers between devices with their start and end apart: 37, of which 18 were waited for; matrix products, arithmetic and copies ran while one was open for 2% of the time, Pallas kernels for 0%

profile of v1, /device:TPU:2, one launch (start us, length us, event | category | flops | bytes accessed | tf_op | source)
XLA Modules:
  0.0 261.4 jit_solution(2963188655079253780)
XLA Ops:
  1.6 3.8 %collective-permute-start = (f32[4,1,512]{2,1,0:T(1,128)S(1)}, f32[4,1,512]{2,1,0:T(1,128)S(1)}, u32[]{:S(2)}, u32[]{:S(2)}) collective-permute-start(f32[4,1,512]{2,1,0:T(1,128)S(1)} %get-tuple-element.324), channel_id=1, source_target_pairs={{0,1},{1,2},{2,3},{3,4},{4,5},{5,6},{6,7},{7,8},{8,9},{9,10},{10,1... | collective-permute-start | bytes 24584 | tf_op jit(solution)/shard_map/ppermute | solution.py:21
  5.4 5.8 %collective-permute-start.1 = (f32[4,1,512]{2,1,0:T(1,128)S(1)}, f32[4,1,512]{2,1,0:T(1,128)S(1)}, u32[]{:S(2)}, u32[]{:S(2)}) collective-permute-start(f32[4,1,512]{2,1,0:T(1,128)S(1)} %get-tuple-element.325), channel_id=1, source_target_pairs={{1,0},{2,1},{3,2},{4,3},{5,4},{6,5},{7,6},{8,7},{9,8},{10,9},{11,1... | collective-permute-start | bytes 24584 | tf_op jit(solution)/shard_map/ppermute | solution.py:23
  19.2 6.0 %collective-permute-start.3 = (f32[4,1,512]{2,1,0:T(1,128)S(1)}, f32[4,1,512]{2,1,0:T(1,128)S(1)}, u32[]{:S(2)}, u32[]{:S(2)}) collective-permute-start(f32[4,1,512]{2,1,0:T(1,128)S(1)} %get-tuple-element.316), channel_id=1, source_target_pairs={{1,0},{2,1},{3,2},{4,3},{5,4},{6,5},{7,6},{8,7},{9,8},{10,9},{11,1... | collective-permute-start | bytes 24584 | tf_op jit(solution)/shard_map/ppermute | solution.py:23
  30.3 5.4 %collective-permute-start.5 = (f32[4,1,512]{2,1,0:T(1,128)S(1)}, f32[4,1,512]{2,1,0:T(1,128)S(1)}, u32[]{:S(2)}, u32[]{:S(2)}) collective-permute-start(f32[4,1,512]{2,1,0:T(1,128)S(1)} %get-tuple-element.307), channel_id=1, source_target_pairs={{1,0},{2,1},{3,2},{4,3},{5,4},{6,5},{7,6},{8,7},{9,8},{10,9},{11,1... | collective-permute-start | bytes 24584 | tf_op jit(solution)/shard_map/ppermute | solution.py:23
  38.0 3.4 %collective-permute-start.6 = (f32[4,1,512]{2,1,0:T(1,128)S(1)}, f32[4,1,512]{2,1,0:T(1,128)S(1)}, u32[]{:S(2)}, u32[]{:S(2)}) collective-permute-start(f32[4,1,512]{2,1,0:T(1,128)S(1)} %get-tuple-element.297), channel_id=1, source_target_pairs={{0,1},{1,2},{2,3},{3,4},{4,5},{5,6},{6,7},{7,8},{8,9},{9,10},{10,1... | collective-permute-start | bytes 24584 | tf_op jit(solution)/shard_map/ppermute | solution.py:21
  41.4 4.8 %collective-permute-start.7 = (f32[4,1,512]{2,1,0:T(1,128)S(1)}, f32[4,1,512]{2,1,0:T(1,128)S(1)}, u32[]{:S(2)}, u32[]{:S(2)}) collective-permute-start(f32[4,1,512]{2,1,0:T(1,128)S(1)} %get-tuple-element.298), channel_id=1, source_target_pairs={{1,0},{2,1},{3,2},{4,3},{5,4},{6,5},{7,6},{8,7},{9,8},{10,9},{11,1... | collective-permute-start | bytes 24584 | tf_op jit(solution)/shard_map/ppermute | solution.py:23
  48.4 3.3 %collective-permute-start.8 = (f32[4,1,512]{2,1,0:T(1,128)S(1)}, f32[4,1,512]{2,1,0:T(1,128)S(1)}, u32[]{:S(2)}, u32[]{:S(2)}) collective-permute-start(f32[4,1,512]{2,1,0:T(1,128)S(1)} %get-tuple-element.288), channel_id=1, source_target_pairs={{0,1},{1,2},{2,3},{3,4},{4,5},{5,6},{6,7},{7,8},{8,9},{9,10},{10,1... | collective-permute-start | bytes 24584 | tf_op jit(solution)/shard_map/ppermute | solution.py:21
  51.7 4.9 %collective-permute-start.9 = (f32[4,1,512]{2,1,0:T(1,128)S(1)}, f32[4,1,512]{2,1,0:T(1,128)S(1)}, u32[]{:S(2)}, u32[]{:S(2)}) collective-permute-start(f32[4,1,512]{2,1,0:T(1,128)S(1)} %get-tuple-element.289), channel_id=1, source_target_pairs={{1,0},{2,1},{3,2},{4,3},{5,4},{6,5},{7,6},{8,7},{9,8},{10,9},{11,1... | collective-permute-start | bytes 24584 | tf_op jit(solution)/shard_map/ppermute | solution.py:23
  61.3 5.8 %collective-permute-start.11 = (f32[4,1,512]{2,1,0:T(1,128)S(1)}, f32[4,1,512]{2,1,0:T(1,128)S(1)}, u32[]{:S(2)}, u32[]{:S(2)}) collective-permute-start(f32[4,1,512]{2,1,0:T(1,128)S(1)} %get-tuple-element.280), channel_id=1, source_target_pairs={{1,0},{2,1},{3,2},{4,3},{5,4},{6,5},{7,6},{8,7},{9,8},{10,9},{11,1... | collective-permute-start | bytes 24584 | tf_op jit(solution)/shard_map/ppermute | solution.py:23
  71.3 6.3 %collective-permute-start.13 = (f32[4,1,512]{2,1,0:T(1,128)S(1)}, f32[4,1,512]{2,1,0:T(1,128)S(1)}, u32[]{:S(2)}, u32[]{:S(2)}) collective-permute-start(f32[4,1,512]{2,1,0:T(1,128)S(1)} %get-tuple-element.271), channel_id=1, source_target_pairs={{1,0},{2,1},{3,2},{4,3},{5,4},{6,5},{7,6},{8,7},{9,8},{10,9},{11,1... | collective-permute-start | bytes 24584 | tf_op jit(solution)/shard_map/ppermute | solution.py:23
  81.7 6.3 %collective-permute-start.15 = (f32[4,1,512]{2,1,0:T(1,128)S(1)}, f32[4,1,512]{2,1,0:T(1,128)S(1)}, u32[]{:S(2)}, u32[]{:S(2)}) collective-permute-start(f32[4,1,512]{2,1,0:T(1,128)S(1)} %get-tuple-element.262), channel_id=1, source_target_pairs={{1,0},{2,1},{3,2},{4,3},{5,4},{6,5},{7,6},{8,7},{9,8},{10,9},{11,1... | collective-permute-start | bytes 24584 | tf_op jit(solution)/shard_map/ppermute | solution.py:23
  92.2 6.3 %collective-permute-start.17 = (f32[4,1,512]{2,1,0:T(1,128)S(1)}, f32[4,1,512]{2,1,0:T(1,128)S(1)}, u32[]{:S(2)}, u32[]{:S(2)}) collective-permute-start(f32[4,1,512]{2,1,0:T(1,128)S(1)} %get-tuple-element.253), channel_id=1, source_target_pairs={{1,0},{2,1},{3,2},{4,3},{5,4},{6,5},{7,6},{8,7},{9,8},{10,9},{11,1... | collective-permute-start | bytes 24584 | tf_op jit(solution)/shard_map/ppermute | solution.py:23
  103.4 6.6 %all-to-all-start = ((f32[16,1,4,32,512]{4,3,2,1,0:T(8,128)}), f32[16,1,4,32,512]{4,3,2,1,0:T(8,128)}, u32[]{:S(2)}, u32[]{:S(2)}) async-start(f32[16,1,4,32,512]{4,3,2,1,0:T(8,128)} %stack.459), calls=%async_computation | async-start | bytes 8388608 | tf_op jit(solution)/shard_map/all_to_all | solution.py:95
  113.3 36.9 %psum.7 = f32[]{:T(128)} all-reduce(f32[]{:T(128)} %fusion.151), channel_id=1, replica_groups=mesh['member'=16,'domain'=16] {'domain'}, use_global_device_ids=true, to_apply=%region_1.2 | all-reduce | flops 1 | bytes 8 | tf_op jit(solution)/shard_map/psum | solution.py:92
  150.9 11.6 %all-to-all-done = f32[16,1,4,32,512]{4,3,2,1,0:T(8,128)} async-done(((f32[16,1,4,32,512]{4,3,2,1,0:T(8,128)}), f32[16,1,4,32,512]{4,3,2,1,0:T(8,128)}, u32[]{:S(2)}, u32[]{:S(2)}) %all-to-all-start) | async-done | bytes 4194336 | tf_op jit(solution)/shard_map/all_to_all | solution.py:95
  165.6 6.9 %collective-permute-start.19 = (f32[4,1,512]{2,1,0:T(1,128)S(1)}, f32[4,1,512]{2,1,0:T(1,128)S(1)}, u32[]{:S(2)}, u32[]{:S(2)}) collective-permute-start(f32[4,1,512]{2,1,0:T(1,128)S(1)} %get-tuple-element.244), channel_id=1, source_target_pairs={{1,0},{2,1},{3,2},{4,3},{5,4},{6,5},{7,6},{8,7},{9,8},{10,9},{11,1... | collective-permute-start | bytes 24584 | tf_op jit(solution)/shard_map/ppermute | solution.py:23
  176.7 6.3 %collective-permute-start.21 = (f32[4,1,512]{2,1,0:T(1,128)S(1)}, f32[4,1,512]{2,1,0:T(1,128)S(1)}, u32[]{:S(2)}, u32[]{:S(2)}) collective-permute-start(f32[4,1,512]{2,1,0:T(1,128)S(1)} %get-tuple-element.235), channel_id=1, source_target_pairs={{1,0},{2,1},{3,2},{4,3},{5,4},{6,5},{7,6},{8,7},{9,8},{10,9},{11,1... | collective-permute-start | bytes 24584 | tf_op jit(solution)/shard_map/ppermute | solution.py:23
  187.1 6.3 %collective-permute-start.23 = (f32[4,1,512]{2,1,0:T(1,128)S(1)}, f32[4,1,512]{2,1,0:T(1,128)S(1)}, u32[]{:S(2)}, u32[]{:S(2)}) collective-permute-start(f32[4,1,512]{2,1,0:T(1,128)S(1)} %get-tuple-element.226), channel_id=1, source_target_pairs={{1,0},{2,1},{3,2},{4,3},{5,4},{6,5},{7,6},{8,7},{9,8},{10,9},{11,1... | collective-permute-start | bytes 24584 | tf_op jit(solution)/shard_map/ppermute | solution.py:23
  197.7 6.3 %collective-permute-start.25 = (f32[4,1,512]{2,1,0:T(1,128)S(1)}, f32[4,1,512]{2,1,0:T(1,128)S(1)}, u32[]{:S(2)}, u32[]{:S(2)}) collective-permute-start(f32[4,1,512]{2,1,0:T(1,128)S(1)} %get-tuple-element.217), channel_id=1, source_target_pairs={{1,0},{2,1},{3,2},{4,3},{5,4},{6,5},{7,6},{8,7},{9,8},{10,9},{11,1... | collective-permute-start | bytes 24584 | tf_op jit(solution)/shard_map/ppermute | solution.py:23
  208.1 6.5 %collective-permute-start.27 = (f32[4,1,512]{2,1,0:T(1,128)S(1)}, f32[4,1,512]{2,1,0:T(1,128)S(1)}, u32[]{:S(2)}, u32[]{:S(2)}) collective-permute-start(f32[4,1,512]{2,1,0:T(1,128)S(1)} %get-tuple-element.208), channel_id=1, source_target_pairs={{1,0},{2,1},{3,2},{4,3},{5,4},{6,5},{7,6},{8,7},{9,8},{10,9},{11,1... | collective-permute-start | bytes 24584 | tf_op jit(solution)/shard_map/ppermute | solution.py:23
  218.5 6.3 %collective-permute-start.29 = (f32[4,1,512]{2,1,0:T(1,128)S(1)}, f32[4,1,512]{2,1,0:T(1,128)S(1)}, u32[]{:S(2)}, u32[]{:S(2)}) collective-permute-start(f32[4,1,512]{2,1,0:T(1,128)S(1)} %get-tuple-element.199), channel_id=1, source_target_pairs={{1,0},{2,1},{3,2},{4,3},{5,4},{6,5},{7,6},{8,7},{9,8},{10,9},{11,1... | collective-permute-start | bytes 24584 | tf_op jit(solution)/shard_map/ppermute | solution.py:23
  229.0 6.3 %collective-permute-start.31 = (f32[4,1,512]{2,1,0:T(1,128)S(1)}, f32[4,1,512]{2,1,0:T(1,128)S(1)}, u32[]{:S(2)}, u32[]{:S(2)}) collective-permute-start(f32[4,1,512]{2,1,0:T(1,128)S(1)} %get-tuple-element.190), channel_id=1, source_target_pairs={{1,0},{2,1},{3,2},{4,3},{5,4},{6,5},{7,6},{8,7},{9,8},{10,9},{11,1... | collective-permute-start | bytes 24584 | tf_op jit(solution)/shard_map/ppermute | solution.py:23
  239.4 6.3 %collective-permute-start.33 = (f32[4,1,512]{2,1,0:T(1,128)S(1)}, f32[4,1,512]{2,1,0:T(1,128)S(1)}, u32[]{:S(2)}, u32[]{:S(2)}) collective-permute-start(f32[4,1,512]{2,1,0:T(1,128)S(1)} %get-tuple-element.181), channel_id=1, source_target_pairs={{1,0},{2,1},{3,2},{4,3},{5,4},{6,5},{7,6},{8,7},{9,8},{10,9},{11,1... | collective-permute-start | bytes 24584 | tf_op jit(solution)/shard_map/ppermute | solution.py:23
  249.9 6.3 %collective-permute-start.35 = (f32[4,1,512]{2,1,0:T(1,128)S(1)}, f32[4,1,512]{2,1,0:T(1,128)S(1)}, u32[]{:S(2)}, u32[]{:S(2)}) collective-permute-start(f32[4,1,512]{2,1,0:T(1,128)S(1)} %get-tuple-element.172), channel_id=1, source_target_pairs={{1,0},{2,1},{3,2},{4,3},{5,4},{6,5},{7,6},{8,7},{9,8},{10,9},{11,1... | collective-permute-start | bytes 24584 | tf_op jit(solution)/shard_map/ppermute | solution.py:23
  (243 shorter events, 80.8 us)
Async XLA Ops:
  1.6 12.7 %collective-permute-start = (f32[4,1,512]{2,1,0:T(1,128)S(1)}, f32[4,1,512]{2,1,0:T(1,128)S(1)}, u32[]{:S(2)}, u32[]{:S(2)}) collective-permute-start(f32[4,1,512]{2,1,0:T(1,128)S(1)} %get-tuple-element.324), channel_id=1, source_target_pairs={{0,1},{1,2},{2,3},{3,4},{4,5},{5,6},{6,7},{7,8},{8,9},{9,10},{10,1... | collective-permute-start | bytes 24584 | tf_op jit(solution)/shard_map/ppermute | solution.py:21
  5.4 8.9 %collective-permute-start.1 = (f32[4,1,512]{2,1,0:T(1,128)S(1)}, f32[4,1,512]{2,1,0:T(1,128)S(1)}, u32[]{:S(2)}, u32[]{:S(2)}) collective-permute-start(f32[4,1,512]{2,1,0:T(1,128)S(1)} %get-tuple-element.325), channel_id=1, source_target_pairs={{1,0},{2,1},{3,2},{4,3},{5,4},{6,5},{7,6},{8,7},{9,8},{10,9},{11,1... | collective-permute-start | bytes 24584 | tf_op jit(solution)/shard_map/ppermute | solution.py:23
  17.2 8.1 %collective-permute-start.2 = (f32[4,1,512]{2,1,0:T(1,128)S(1)}, f32[4,1,512]{2,1,0:T(1,128)S(1)}, u32[]{:S(2)}, u32[]{:S(2)}) collective-permute-start(f32[4,1,512]{2,1,0:T(1,128)S(1)} %get-tuple-element.315), channel_id=1, source_target_pairs={{0,1},{1,2},{2,3},{3,4},{4,5},{5,6},{6,7},{7,8},{8,9},{9,10},{10,1... | collective-permute-start | bytes 24584 | tf_op jit(solution)/shard_map/ppermute | solution.py:21
  27.4 8.3 %collective-permute-start.4 = (f32[4,1,512]{2,1,0:T(1,128)S(1)}, f32[4,1,512]{2,1,0:T(1,128)S(1)}, u32[]{:S(2)}, u32[]{:S(2)}) collective-permute-start(f32[4,1,512]{2,1,0:T(1,128)S(1)} %get-tuple-element.306), channel_id=1, source_target_pairs={{0,1},{1,2},{2,3},{3,4},{4,5},{5,6},{6,7},{7,8},{8,9},{9,10},{10,1... | collective-permute-start | bytes 24584 | tf_op jit(solution)/shard_map/ppermute | solution.py:21
  38.0 8.3 %collective-permute-start.6 = (f32[4,1,512]{2,1,0:T(1,128)S(1)}, f32[4,1,512]{2,1,0:T(1,128)S(1)}, u32[]{:S(2)}, u32[]{:S(2)}) collective-permute-start(f32[4,1,512]{2,1,0:T(1,128)S(1)} %get-tuple-element.297), channel_id=1, source_target_pairs={{0,1},{1,2},{2,3},{3,4},{4,5},{5,6},{6,7},{7,8},{8,9},{9,10},{10,1... | collective-permute-start | bytes 24584 | tf_op jit(solution)/shard_map/ppermute | solution.py:21
  48.4 8.3 %collective-permute-start.8 = (f32[4,1,512]{2,1,0:T(1,128)S(1)}, f32[4,1,512]{2,1,0:T(1,128)S(1)}, u32[]{:S(2)}, u32[]{:S(2)}) collective-permute-start(f32[4,1,512]{2,1,0:T(1,128)S(1)} %get-tuple-element.288), channel_id=1, source_target_pairs={{0,1},{1,2},{2,3},{3,4},{4,5},{5,6},{6,7},{7,8},{8,9},{9,10},{10,1... | collective-permute-start | bytes 24584 | tf_op jit(solution)/shard_map/ppermute | solution.py:21
  58.8 8.3 %collective-permute-start.10 = (f32[4,1,512]{2,1,0:T(1,128)S(1)}, f32[4,1,512]{2,1,0:T(1,128)S(1)}, u32[]{:S(2)}, u32[]{:S(2)}) collective-permute-start(f32[4,1,512]{2,1,0:T(1,128)S(1)} %get-tuple-element.279), channel_id=1, source_target_pairs={{0,1},{1,2},{2,3},{3,4},{4,5},{5,6},{6,7},{7,8},{8,9},{9,10},{10,1... | collective-permute-start | bytes 24584 | tf_op jit(solution)/shard_map/ppermute | solution.py:21
  69.4 8.3 %collective-permute-start.12 = (f32[4,1,512]{2,1,0:T(1,128)S(1)}, f32[4,1,512]{2,1,0:T(1,128)S(1)}, u32[]{:S(2)}, u32[]{:S(2)}) collective-permute-start(f32[4,1,512]{2,1,0:T(1,128)S(1)} %get-tuple-element.270), channel_id=1, source_target_pairs={{0,1},{1,2},{2,3},{3,4},{4,5},{5,6},{6,7},{7,8},{8,9},{9,10},{10,1... | collective-permute-start | bytes 24584 | tf_op jit(solution)/shard_map/ppermute | solution.py:21
  71.3 7.7 %collective-permute-start.13 = (f32[4,1,512]{2,1,0:T(1,128)S(1)}, f32[4,1,512]{2,1,0:T(1,128)S(1)}, u32[]{:S(2)}, u32[]{:S(2)}) collective-permute-start(f32[4,1,512]{2,1,0:T(1,128)S(1)} %get-tuple-element.271), channel_id=1, source_target_pairs={{1,0},{2,1},{3,2},{4,3},{5,4},{6,5},{7,6},{8,7},{9,8},{10,9},{11,1... | collective-permute-start | bytes 24584 | tf_op jit(solution)/shard_map/ppermute | solution.py:23
  79.8 8.3 %collective-permute-start.14 = (f32[4,1,512]{2,1,0:T(1,128)S(1)}, f32[4,1,512]{2,1,0:T(1,128)S(1)}, u32[]{:S(2)}, u32[]{:S(2)}) collective-permute-start(f32[4,1,512]{2,1,0:T(1,128)S(1)} %get-tuple-element.261), channel_id=1, source_target_pairs={{0,1},{1,2},{2,3},{3,4},{4,5},{5,6},{6,7},{7,8},{8,9},{9,10},{10,1... | collective-permute-start | bytes 24584 | tf_op jit(solution)/shard_map/ppermute | solution.py:21
  81.7 7.7 %collective-permute-start.15 = (f32[4,1,512]{2,1,0:T(1,128)S(1)}, f32[4,1,512]{2,1,0:T(1,128)S(1)}, u32[]{:S(2)}, u32[]{:S(2)}) collective-permute-start(f32[4,1,512]{2,1,0:T(1,128)S(1)} %get-tuple-element.262), channel_id=1, source_target_pairs={{1,0},{2,1},{3,2},{4,3},{5,4},{6,5},{7,6},{8,7},{9,8},{10,9},{11,1... | collective-permute-start | bytes 24584 | tf_op jit(solution)/shard_map/ppermute | solution.py:23
  90.2 8.3 %collective-permute-start.16 = (f32[4,1,512]{2,1,0:T(1,128)S(1)}, f32[4,1,512]{2,1,0:T(1,128)S(1)}, u32[]{:S(2)}, u32[]{:S(2)}) collective-permute-start(f32[4,1,512]{2,1,0:T(1,128)S(1)} %get-tuple-element.252), channel_id=1, source_target_pairs={{0,1},{1,2},{2,3},{3,4},{4,5},{5,6},{6,7},{7,8},{8,9},{9,10},{10,1... | collective-permute-start | bytes 24584 | tf_op jit(solution)/shard_map/ppermute | solution.py:21
  92.2 7.7 %collective-permute-start.17 = (f32[4,1,512]{2,1,0:T(1,128)S(1)}, f32[4,1,512]{2,1,0:T(1,128)S(1)}, u32[]{:S(2)}, u32[]{:S(2)}) collective-permute-start(f32[4,1,512]{2,1,0:T(1,128)S(1)} %get-tuple-element.253), channel_id=1, source_target_pairs={{1,0},{2,1},{3,2},{4,3},{5,4},{6,5},{7,6},{8,7},{9,8},{10,9},{11,1... | collective-permute-start | bytes 24584 | tf_op jit(solution)/shard_map/ppermute | solution.py:23
  103.4 59.0 %all-to-all-start = ((f32[16,1,4,32,512]{4,3,2,1,0:T(8,128)}), f32[16,1,4,32,512]{4,3,2,1,0:T(8,128)}, u32[]{:S(2)}, u32[]{:S(2)}) async-start(f32[16,1,4,32,512]{4,3,2,1,0:T(8,128)} %stack.459), calls=%async_computation | async-start | bytes 8388608 | tf_op jit(solution)/shard_map/all_to_all | solution.py:95
  163.7 8.9 %collective-permute-start.18 = (f32[4,1,512]{2,1,0:T(1,128)S(1)}, f32[4,1,512]{2,1,0:T(1,128)S(1)}, u32[]{:S(2)}, u32[]{:S(2)}) collective-permute-start(f32[4,1,512]{2,1,0:T(1,128)S(1)} %get-tuple-element.243), channel_id=1, source_target_pairs={{0,1},{1,2},{2,3},{3,4},{4,5},{5,6},{6,7},{7,8},{8,9},{9,10},{10,1... | collective-permute-start | bytes 24584 | tf_op jit(solution)/shard_map/ppermute | solution.py:21
  165.6 8.3 %collective-permute-start.19 = (f32[4,1,512]{2,1,0:T(1,128)S(1)}, f32[4,1,512]{2,1,0:T(1,128)S(1)}, u32[]{:S(2)}, u32[]{:S(2)}) collective-permute-start(f32[4,1,512]{2,1,0:T(1,128)S(1)} %get-tuple-element.244), channel_id=1, source_target_pairs={{1,0},{2,1},{3,2},{4,3},{5,4},{6,5},{7,6},{8,7},{9,8},{10,9},{11,1... | collective-permute-start | bytes 24584 | tf_op jit(solution)/shard_map/ppermute | solution.py:23
  174.7 8.3 %collective-permute-start.20 = (f32[4,1,512]{2,1,0:T(1,128)S(1)}, f32[4,1,512]{2,1,0:T(1,128)S(1)}, u32[]{:S(2)}, u32[]{:S(2)}) collective-permute-start(f32[4,1,512]{2,1,0:T(1,128)S(1)} %get-tuple-element.234), channel_id=1, source_target_pairs={{0,1},{1,2},{2,3},{3,4},{4,5},{5,6},{6,7},{7,8},{8,9},{9,10},{10,1... | collective-permute-start | bytes 24584 | tf_op jit(solution)/shard_map/ppermute | solution.py:21
  185.2 8.3 %collective-permute-start.22 = (f32[4,1,512]{2,1,0:T(1,128)S(1)}, f32[4,1,512]{2,1,0:T(1,128)S(1)}, u32[]{:S(2)}, u32[]{:S(2)}) collective-permute-start(f32[4,1,512]{2,1,0:T(1,128)S(1)} %get-tuple-element.225), channel_id=1, source_target_pairs={{0,1},{1,2},{2,3},{3,4},{4,5},{5,6},{6,7},{7,8},{8,9},{9,10},{10,1... | collective-permute-start | bytes 24584 | tf_op jit(solution)/shard_map/ppermute | solution.py:21
  195.7 8.3 %collective-permute-start.24 = (f32[4,1,512]{2,1,0:T(1,128)S(1)}, f32[4,1,512]{2,1,0:T(1,128)S(1)}, u32[]{:S(2)}, u32[]{:S(2)}) collective-permute-start(f32[4,1,512]{2,1,0:T(1,128)S(1)} %get-tuple-element.216), channel_id=1, source_target_pairs={{0,1},{1,2},{2,3},{3,4},{4,5},{5,6},{6,7},{7,8},{8,9},{9,10},{10,1... | collective-permute-start | bytes 24584 | tf_op jit(solution)/shard_map/ppermute | solution.py:21
  206.2 8.5 %collective-permute-start.26 = (f32[4,1,512]{2,1,0:T(1,128)S(1)}, f32[4,1,512]{2,1,0:T(1,128)S(1)}, u32[]{:S(2)}, u32[]{:S(2)}) collective-permute-start(f32[4,1,512]{2,1,0:T(1,128)S(1)} %get-tuple-element.207), channel_id=1, source_target_pairs={{0,1},{1,2},{2,3},{3,4},{4,5},{5,6},{6,7},{7,8},{8,9},{9,10},{10,1... | collective-permute-start | bytes 24584 | tf_op jit(solution)/shard_map/ppermute | solution.py:21
  216.6 8.3 %collective-permute-start.28 = (f32[4,1,512]{2,1,0:T(1,128)S(1)}, f32[4,1,512]{2,1,0:T(1,128)S(1)}, u32[]{:S(2)}, u32[]{:S(2)}) collective-permute-start(f32[4,1,512]{2,1,0:T(1,128)S(1)} %get-tuple-element.198), channel_id=1, source_target_pairs={{0,1},{1,2},{2,3},{3,4},{4,5},{5,6},{6,7},{7,8},{8,9},{9,10},{10,1... | collective-permute-start | bytes 24584 | tf_op jit(solution)/shard_map/ppermute | solution.py:21
  227.1 8.3 %collective-permute-start.30 = (f32[4,1,512]{2,1,0:T(1,128)S(1)}, f32[4,1,512]{2,1,0:T(1,128)S(1)}, u32[]{:S(2)}, u32[]{:S(2)}) collective-permute-start(f32[4,1,512]{2,1,0:T(1,128)S(1)} %get-tuple-element.189), channel_id=1, source_target_pairs={{0,1},{1,2},{2,3},{3,4},{4,5},{5,6},{6,7},{7,8},{8,9},{9,10},{10,1... | collective-permute-start | bytes 24584 | tf_op jit(solution)/shard_map/ppermute | solution.py:21
  237.5 8.3 %collective-permute-start.32 = (f32[4,1,512]{2,1,0:T(1,128)S(1)}, f32[4,1,512]{2,1,0:T(1,128)S(1)}, u32[]{:S(2)}, u32[]{:S(2)}) collective-permute-start(f32[4,1,512]{2,1,0:T(1,128)S(1)} %get-tuple-element.180), channel_id=1, source_target_pairs={{0,1},{1,2},{2,3},{3,4},{4,5},{5,6},{6,7},{7,8},{8,9},{9,10},{10,1... | collective-permute-start | bytes 24584 | tf_op jit(solution)/shard_map/ppermute | solution.py:21
  248.0 8.3 %collective-permute-start.34 = (f32[4,1,512]{2,1,0:T(1,128)S(1)}, f32[4,1,512]{2,1,0:T(1,128)S(1)}, u32[]{:S(2)}, u32[]{:S(2)}) collective-permute-start(f32[4,1,512]{2,1,0:T(1,128)S(1)} %get-tuple-element.171), channel_id=1, source_target_pairs={{0,1},{1,2},{2,3},{3,4},{4,5},{5,6},{6,7},{7,8},{8,9},{9,10},{10,1... | collective-permute-start | bytes 24584 | tf_op jit(solution)/shard_map/ppermute | solution.py:21
  (16 other events, 176.9 us)
